TPU v7x, 32 devices: a whole 2x2x4 slice. The times are simulated.
32 devices in a mesh: groups: 2 (over y), seq: 4 (over z), dp: 2 (over x), mp: 2 (over core).
Axes of the slice: x: 2, y: 2, z: 4, core: 2. Of those that a mesh axis runs over, the one named last changes fastest.
Arguments:
- queries: bfloat16 [4, 512, 2048], P(('groups', 'dp'), 'seq', 'mp'), parts along dimension 0, may hold values from -6 to 6
- keys: bfloat16 [4, 512, 2048], P(('groups', 'dp'), 'seq', 'mp'), parts along dimension 0, may hold values from -6 to 6
- values: bfloat16 [4, 512, 2048], P(('groups', 'dp'), 'seq', 'mp'), parts along dimension 0, may hold values from -6 to 6
- grad_output: bfloat16 [4, 512, 2048], P(('groups', 'dp'), 'seq', 'mp'), parts along dimension 0, may hold values from -6 to 6
- counts: int32 [4, 4, 4], P(('groups', 'dp'), 'seq'), parts along dimension 0, may hold values from 0 to 64, as said below
Outputs:
- grad_queries: bfloat16 [4, 512, 2048], P(('groups', 'dp'), 'seq', 'mp'), parts along dimension 0
- grad_keys: bfloat16 [4, 512, 2048], P(('groups', 'dp'), 'seq', 'mp'), parts along dimension 0
- grad_values: bfloat16 [4, 512, 2048], P(('groups', 'dp'), 'seq', 'mp'), parts along dimension 0
There are 2 independent parts, one for each index of `groups`. A program takes and returns all parts, laid end to end along the dimension named above; each array names one. Nothing has to cross between parts.
Inputs may be any that keep to these rules, and one draw needn't show every extreme that they name: Each shard's counts sum to 128; no entry exceeds 64, some window receives 64 points from every shard.
All inputs are finite; a program needn't handle non-finite values.
Results may differ from a plain program's by a relative error of at most 0.001.
Values may be sent and summed in bfloat16 or wider, within the bound.
A program may use at most 128 MiB of HBM per device.

v0:
```python
import math
import jax
import jax.numpy as jnp
from jax import lax
from jax.sharding import PartitionSpec as P

DH = 128
highest = lax.Precision.HIGHEST


def entering(value, axis, join, neutral, backward):
    count, mine = (lax.axis_size(axis), lax.axis_index(axis))
    pieces = lax.all_gather(value, axis)
    if backward:
        pieces = pieces[::-1]
        mine = count - 1 - mine
    total = jnp.full_like(value, 0) + jnp.asarray(neutral, value.dtype)

    def hop(position, total):
        longer = join(total, pieces[position])
        return jnp.where(position < mine, longer, total)

    return lax.fori_loop(0, count - 1, hop, total)


def add_states(earlier, later):
    return earlier + later


def per_device(queries, keys, values, grad_output, counts):
    shard_count = lax.axis_size("seq")
    local_rows = queries.shape[1]
    width = queries.shape[2]
    local_heads = width // DH
    capacity = 2 * local_rows // shard_count
    window_rows = shard_count * capacity
    factor = 1.0 / math.sqrt(DH * local_rows * shard_count)
    my_counts = counts[0, 0]
    window_ends = jnp.cumsum(my_counts)
    window_starts = window_ends - my_counts
    offsets = jnp.arange(capacity, dtype=jnp.int32)
    occupied = offsets[None, :] < my_counts[:, None]
    picked = jnp.where(occupied, window_starts[:, None] + offsets[None, :], 0).reshape(-1)
    occupied_column = occupied.reshape(-1, 1)

    def pack(source):
        taken = jnp.take(source[0], picked, axis=0)
        taken = jnp.where(occupied_column, taken, jnp.zeros_like(taken))
        return taken.reshape(shard_count, capacity, width)

    def split_heads(received):
        return received.reshape(window_rows, local_heads, DH)

    def outer_sum(left, right):
        return jnp.einsum("lha,lhb->hab", left, right, preferred_element_type=jnp.float32)

    query_recv, key_recv, value_recv, grad_recv = (
        lax.all_to_all(pack(queries), "seq", split_axis=0, concat_axis=0, tiled=True),
        lax.all_to_all(pack(keys), "seq", split_axis=0, concat_axis=0, tiled=True),
        lax.all_to_all(pack(values), "seq", split_axis=0, concat_axis=0, tiled=True),
        lax.all_to_all(pack(grad_output), "seq", split_axis=0, concat_axis=0, tiled=True),
    )
    query_recv = split_heads(query_recv)
    key_recv = split_heads(key_recv)
    value_recv = split_heads(value_recv)
    grad_recv = split_heads(grad_recv)
    key_state = outer_sum(key_recv, value_recv)
    query_state = outer_sum(query_recv, grad_recv)
    zero_state = jnp.zeros((local_heads, DH, DH), jnp.float32)
    before_kv = entering(key_state, "seq", add_states, zero_state, False)
    after_qd = entering(query_state, "seq", add_states, zero_state, True)
    block = min(512, window_rows)
    nblocks = window_rows // block

    def blocked(received):
        return received.reshape(nblocks, block, local_heads, DH)

    query_blocks = blocked(query_recv)
    key_blocks = blocked(key_recv)
    value_blocks = blocked(value_recv)
    grad_blocks = blocked(grad_recv)
    block_kv = jnp.einsum(
        "nlha,nlhb->nhab", key_blocks, value_blocks, preferred_element_type=jnp.float32
    )
    block_qd = jnp.einsum(
        "nlha,nlhb->nhab", query_blocks, grad_blocks, preferred_element_type=jnp.float32
    )
    kv_before = before_kv[None] + jnp.cumsum(block_kv, axis=0) - block_kv
    qd_after = after_qd[None] + jnp.sum(block_qd, axis=0)[None] - jnp.cumsum(block_qd, axis=0)
    lower = (
        lax.broadcasted_iota(jnp.int32, (block, block), 0)
        >= lax.broadcasted_iota(jnp.int32, (block, block), 1)
    ).astype(jnp.float32)

    def one_block(pieces):
        query_part, key_part, value_part, grad_part, kv_state, qd_state = pieces
        weights = (
            jnp.einsum("rha,sha->hrs", grad_part, value_part, preferred_element_type=jnp.float32)
            * lower[None]
        )
        scores = (
            jnp.einsum("rha,sha->hrs", query_part, key_part, preferred_element_type=jnp.float32)
            * lower[None]
        )
        query_f = query_part.astype(jnp.float32)
        key_f = key_part.astype(jnp.float32)
        value_f = value_part.astype(jnp.float32)
        grad_f = grad_part.astype(jnp.float32)
        grad_q = jnp.einsum("rhb,hab->rha", grad_f, kv_state, precision=highest) + jnp.einsum(
            "hrs,sha->rha", weights, key_f, precision=highest
        )
        grad_k = jnp.einsum("shb,hab->sha", value_f, qd_state, precision=highest) + jnp.einsum(
            "hrs,rha->sha", weights, query_f, precision=highest
        )
        grad_v = jnp.einsum("sha,hab->shb", key_f, qd_state, precision=highest) + jnp.einsum(
            "hrs,rhb->shb", scores, grad_f, precision=highest
        )

        def finish(result):
            return (result * factor).astype(jnp.bfloat16).reshape(block, width)

        return (finish(grad_q), finish(grad_k), finish(grad_v))

    out_q, out_k, out_v = lax.map(
        one_block, (query_blocks, key_blocks, value_blocks, grad_blocks, kv_before, qd_after)
    )

    def to_slots(result):
        return result.reshape(shard_count, capacity, width)

    back_q, back_k, back_v = (
        lax.all_to_all(to_slots(out_q), "seq", split_axis=0, concat_axis=0, tiled=True),
        lax.all_to_all(to_slots(out_k), "seq", split_axis=0, concat_axis=0, tiled=True),
        lax.all_to_all(to_slots(out_v), "seq", split_axis=0, concat_axis=0, tiled=True),
    )
    positions = jnp.arange(local_rows, dtype=jnp.int32)
    member = (
        (positions[:, None] >= window_starts[None, :]) & (positions[:, None] < window_ends[None, :])
    ).astype(jnp.int32)
    window_of = jnp.sum(member * jnp.arange(shard_count, dtype=jnp.int32)[None, :], axis=1)
    start_of = jnp.sum(member * window_starts[None, :], axis=1)
    source_index = window_of * capacity + positions - start_of

    def unpack(returned):
        return jnp.take(returned.reshape(window_rows, width), source_index, axis=0)[None]

    return (unpack(back_q), unpack(back_k), unpack(back_v))


def solution(mesh):
    placed = (
        P(("groups", "dp"), "seq", "mp"),
        P(("groups", "dp"), "seq", "mp"),
        P(("groups", "dp"), "seq", "mp"),
        P(("groups", "dp"), "seq", "mp"),
        P(("groups", "dp"), "seq", None),
    )
    return jax.shard_map(
        per_device,
        mesh=mesh,
        in_specs=placed,
        out_specs=(
            P(("groups", "dp"), "seq", "mp"),
            P(("groups", "dp"), "seq", "mp"),
            P(("groups", "dp"), "seq", "mp"),
        ),
        check_vma=False,
    )
```

profile of v0, /device:TPU:0, one launch (start us, length us, event | category | flops | bytes accessed | tf_op | source)
XLA Modules:
  0.0 218.9 jit_solution(3963657289021872831)
XLA Ops:
  7.2 0.0 copy-start
  7.2 0.8 iota_compare_fusion.3
  8.0 0.1 lt.87
  8.0 0.8 reduce-window.7
  8.9 0.7 bitcast_subtract_fusion
  9.5 0.1 iota_add_fusion
  9.6 0.1 add.117
  9.7 0.0 copy-start.1
  9.7 1.2 gather_fusion.4
  10.9 1.2 gather_fusion.1
  12.1 1.2 gather_fusion.2
  13.3 1.2 gather_fusion
  14.5 1.3 select_select_fusion
  15.8 20.6 %all_to_all.35 = bf16[4,64,1024]{2,1,0:T(8,128)(2,1)S(1)} all-to-all(bf16[4,64,1024]{2,1,0:T(8,128)(2,1)S(1)} %bitcast.68), channel_id=1, replica_groups=mesh['groups'=2,'seq'=4,'dp'=2,'mp'=2] {'seq'}, dimensions={0} | all-to-all | bytes 1048576 | tf_op jit(solution)/shard_map/all_to_all | solution.py:61
  36.4 3.5 %all-to-all-start.4 = ((bf16[4,64,1024]{2,1,0:T(8,128)(2,1)}), bf16[4,64,1024]{2,1,0:T(8,128)(2,1)S(1)}, u32[]{:S(2)}, u32[]{:S(2)}) async-start(bf16[4,64,1024]{2,1,0:T(8,128)(2,1)} %bitcast.14), calls=%async_computation.4 | async-start | bytes 1048576 | tf_op jit(solution)/shard_map/all_to_all | solution.py:58
  39.9 0.0 all-gather.7.cloned.1.call-start
  39.9 0.1 copy.71
  40.0 0.3 copy.66
  40.4 13.1 %all-to-all-done.4 = bf16[4,64,1024]{2,1,0:T(8,128)(2,1)S(1)} async-done(((bf16[4,64,1024]{2,1,0:T(8,128)(2,1)}), bf16[4,64,1024]{2,1,0:T(8,128)(2,1)S(1)}, u32[]{:S(2)}, u32[]{:S(2)}) %all-to-all-start.4) | async-done | bytes 524320 | tf_op jit(solution)/shard_map/all_to_all | solution.py:58
  53.5 0.1 copy.72
  53.6 1.2 fusion.47
  54.7 0.0 all-gather.7.cloned.1.call-update
  54.8 27.9 %all_to_all.36 = bf16[4,64,1024]{2,1,0:T(8,128)(2,1)S(1)} all-to-all(bf16[4,64,1024]{2,1,0:T(8,128)(2,1)S(1)} %bitcast.67), channel_id=1, replica_groups=mesh['groups'=2,'seq'=4,'dp'=2,'mp'=2] {'seq'}, dimensions={0} | all-to-all | bytes 1048576 | tf_op jit(solution)/shard_map/all_to_all | solution.py:59
  82.7 4.1 %all-to-all-start.1 = ((bf16[4,64,1024]{2,1,0:T(8,128)(2,1)}), bf16[4,64,1024]{2,1,0:T(8,128)(2,1)S(1)}, u32[]{:S(2)}, u32[]{:S(2)}) async-start(bf16[4,64,1024]{2,1,0:T(8,128)(2,1)} %bitcast.6), calls=%async_computation.1 | async-start | bytes 1048576 | tf_op jit(solution)/shard_map/all_to_all | solution.py:60
  86.9 0.1 copy.69
  87.0 25.5 %all-to-all-done.1 = bf16[4,64,1024]{2,1,0:T(8,128)(2,1)S(1)} async-done(((bf16[4,64,1024]{2,1,0:T(8,128)(2,1)}), bf16[4,64,1024]{2,1,0:T(8,128)(2,1)S(1)}, u32[]{:S(2)}, u32[]{:S(2)}) %all-to-all-start.1) | async-done | bytes 524320 | tf_op jit(solution)/shard_map/all_to_all | solution.py:60
  112.4 0.9 copy.70
  113.3 2.2 fusion.55
  115.5 0.0 all-gather.5.cloned.1.call-update
  115.6 1.8 fusion.49
  117.4 3.2 %rev.3 = f32[4,8,128,128]{3,2,1,0:T(8,128)} reverse(f32[4,8,128,128]{3,2,1,0:T(8,128)} %bitcast.69), dimensions={0} | reverse | bytes 4194304 | tf_op jit(solution)/shard_map/rev | solution.py:15
  120.7 3.8 %while.35 = (s32[]{:T(128)}, f32[8,128,128]{2,1,0:T(8,128)S(1)}, s32[]{:T(128)}, f32[4,8,128,128]{3,2,1,0:T(8,128)}, s32[]{:T(128)}, /*index=5*/s32[]{:T(128)}) while((s32[]{:T(128)}, f32[8,128,128]{2,1,0:T(8,128)S(1)}, s32[]{:T(128)}, f32[4,8,128,128]{3,2,1,0:T(8,128)}, s32[]{:T(128)}, /*index=5*/s32[]{:T(128)}) %tuple.75), condition=%wide.region_6.9_spmd.clone, body=%wide.region_5.8_spmd.clone.sunk | while | flops 393220 | bytes 1572965 | solution.py:23
  120.7 1.3 add_select_fusion.5
  122.0 1.2 add_select_fusion.5
  123.2 1.3 add_select_fusion.5
  124.5 0.6 fusion.60
  125.2 1.0 copy-done.12
  126.1 1.1 fusion.39
  127.2 0.3 copy.67
  127.5 1.0 reshape.172
  128.6 4.1 %all-to-all-start.6 = ((bf16[4,64,1024]{2,1,0:T(8,128)(2,1)}), bf16[4,64,1024]{2,1,0:T(8,128)(2,1)}, u32[]{:S(2)}, u32[]{:S(2)}) async-start(bf16[4,64,1024]{2,1,0:T(8,128)(2,1)} %reshape.172), calls=%async_computation.6 | async-start | bytes 1048576 | tf_op jit(solution)/shard_map/all_to_all | solution.py:134
  132.7 1.8 fusion.53
  134.5 1.7 fusion.51
  136.2 1.2 fusion.36
  137.4 1.1 copy.61
  138.5 2.1 reshape.170
  140.6 21.8 %all-to-all-done.6 = bf16[4,64,1024]{2,1,0:T(8,128)(2,1)} async-done(((bf16[4,64,1024]{2,1,0:T(8,128)(2,1)}), bf16[4,64,1024]{2,1,0:T(8,128)(2,1)}, u32[]{:S(2)}, u32[]{:S(2)}) %all-to-all-start.6) | async-done | bytes 524320 | tf_op jit(solution)/shard_map/all_to_all | solution.py:134
  162.4 4.3 %all-to-all-start.5 = ((bf16[4,64,1024]{2,1,0:T(8,128)(2,1)}), bf16[4,64,1024]{2,1,0:T(8,128)(2,1)}, u32[]{:S(2)}, u32[]{:S(2)}) async-start(bf16[4,64,1024]{2,1,0:T(8,128)(2,1)} %reshape.170), calls=%async_computation.5 | async-start | bytes 1048576 | tf_op jit(solution)/shard_map/all_to_all | solution.py:133
  166.7 17.4 %all-gather.5.cloned.1.call-done = f32[32,128,128]{2,1,0:T(8,128)} async-done(((f32[8,128,128]{2,1,0:T(8,128)}), f32[32,128,128]{2,1,0:T(8,128)}) %all-gather.5.cloned.1.call-update) | async-done | bytes 2097168 | tf_op jit(solution)/shard_map/all_gather | solution.py:13
  184.1 3.8 %while.34 = (s32[]{:T(128)}, f32[8,128,128]{2,1,0:T(8,128)S(1)}, s32[]{:T(128)}, f32[4,8,128,128]{3,2,1,0:T(8,128)}, s32[]{:T(128)}, /*index=5*/s32[]{:T(128)}) while((s32[]{:T(128)}, f32[8,128,128]{2,1,0:T(8,128)S(1)}, s32[]{:T(128)}, f32[4,8,128,128]{3,2,1,0:T(8,128)}, s32[]{:T(128)}, /*index=5*/s32[]{:T(128)}) %tuple.85), condition=%wide.region_2.4_spmd.clone, body=%wide.region_1.3_spmd.clone.sunk | while | flops 393220 | bytes 1572965 | solution.py:23
  184.1 1.3 add_select_fusion.4
  185.4 1.2 add_select_fusion.4
  186.7 1.2 add_select_fusion.4
  187.9 1.7 fusion.45
  189.6 1.4 fusion.33
  191.1 0.3 copy.56
  191.4 1.0 reshape.166
  192.5 3.5 %all-to-all-start.3 = ((bf16[4,64,1024]{2,1,0:T(8,128)(2,1)}), bf16[4,64,1024]{2,1,0:T(8,128)(2,1)S(1)}, u32[]{:S(2)}, u32[]{:S(2)}) async-start(bf16[4,64,1024]{2,1,0:T(8,128)(2,1)} %reshape.166), calls=%async_computation.3 | async-start | bytes 1048576 | tf_op jit(solution)/shard_map/all_to_all | solution.py:132
  195.9 0.1 select_reduce_fusion.1
  196.0 2.2 gather_fusion.6
  198.2 2.2 gather_fusion.5
  200.4 9.9 %all-to-all-done.3 = bf16[4,64,1024]{2,1,0:T(8,128)(2,1)S(1)} async-done(((bf16[4,64,1024]{2,1,0:T(8,128)(2,1)}), bf16[4,64,1024]{2,1,0:T(8,128)(2,1)S(1)}, u32[]{:S(2)}, u32[]{:S(2)}) %all-to-all-start.3) | async-done | bytes 524320 | tf_op jit(solution)/shard_map/all_to_all | solution.py:132
  210.2 0.9 gather_fusion.3
  211.1 1.0 select_bitcast_fusion
  (39 shorter events, 0.1 us)
Async XLA Ops:
  7.2 2.5 %copy-start = (bf16[1,128,1024]{2,1,0:T(8,128)(2,1)S(1)}, bf16[1,128,1024]{2,1,0:T(8,128)(2,1)}, u32[]{:S(2)}) copy-start(bf16[1,128,1024]{2,1,0:T(8,128)(2,1)} %param.13) | copy-start | bytes 786436
  9.7 1.2 copy-start.1
  10.9 1.2 copy-start.2
  12.1 1.2 copy-start.3
  36.4 17.1 %all-to-all-start.4 = ((bf16[4,64,1024]{2,1,0:T(8,128)(2,1)}), bf16[4,64,1024]{2,1,0:T(8,128)(2,1)S(1)}, u32[]{:S(2)}, u32[]{:S(2)}) async-start(bf16[4,64,1024]{2,1,0:T(8,128)(2,1)} %bitcast.14), calls=%async_computation.4 | async-start | bytes 1048576 | tf_op jit(solution)/shard_map/all_to_all | solution.py:58
  39.9 77.6 %all-gather.7.cloned.1.call-start = ((), (), s32[]{:S(2)}) async-start(), calls=%async_computation.8 | async-start | bytes 2621440 | tf_op jit(solution)/shard_map/all_gather | solution.py:13
  40.3 84.8 %copy-start.4 = (bf16[256,8,128]{0,2,1:T(8,128)(2,1)}, bf16[256,8,128]{0,2,1:T(8,128)(2,1)S(1)}, u32[]{:S(2)}) copy-start(bf16[256,8,128]{0,2,1:T(8,128)(2,1)S(1)} %copy.66) | copy-start | bytes 1572868
  53.6 62.0 %copy-start.10 = (bf16[32,8,8,128]{3,2,1,0:T(8,128)(2,1)}, bf16[32,8,8,128]{3,2,1,0:T(8,128)(2,1)S(1)}, u32[]{:S(2)}) copy-start(bf16[32,8,8,128]{3,2,1,0:T(8,128)(2,1)S(1)} %copy.72) | copy-start | bytes 1572868
  82.7 29.7 %all-to-all-start.1 = ((bf16[4,64,1024]{2,1,0:T(8,128)(2,1)}), bf16[4,64,1024]{2,1,0:T(8,128)(2,1)S(1)}, u32[]{:S(2)}, u32[]{:S(2)}) async-start(bf16[4,64,1024]{2,1,0:T(8,128)(2,1)} %bitcast.6), calls=%async_computation.1 | async-start | bytes 1048576 | tf_op jit(solution)/shard_map/all_to_all | solution.py:60
  86.9 97.3 %all-gather.5.cloned.1.call-start = ((), (), s32[]{:S(2)}) async-start(), calls=%async_computation.7 | async-start | bytes 2621440 | tf_op jit(solution)/shard_map/all_gather | solution.py:13
  87.0 37.5 %copy-start.6 = (bf16[32,8,8,128]{3,2,1,0:T(8,128)(2,1)}, bf16[32,8,8,128]{3,2,1,0:T(8,128)(2,1)S(1)}, u32[]{:S(2)}) copy-start(bf16[32,8,8,128]{3,2,1,0:T(8,128)(2,1)S(1)} %copy.69) | copy-start | bytes 1572868
  115.6 9.5 %copy-start.13 = (f32[256,256]{1,0:T(8,128)}, f32[256,256]{1,0:T(8,128)S(1)}, u32[]{:S(2)}) copy-start(f32[256,256]{1,0:T(8,128)S(1)} %fusion.62) | copy-start | bytes 786436
  120.7 3.9 %copy-start.8 = (f32[8,128,128]{2,1,0:T(8,128)S(1)}, f32[8,128,128]{2,1,0:T(8,128)}, u32[]{:S(2)}) copy-start(f32[8,128,128]{2,1,0:T(8,128)} %fusion.47) | copy-start | bytes 1572868
  124.5 1.7 copy-start.12
  128.6 33.8 %all-to-all-start.6 = ((bf16[4,64,1024]{2,1,0:T(8,128)(2,1)}), bf16[4,64,1024]{2,1,0:T(8,128)(2,1)}, u32[]{:S(2)}, u32[]{:S(2)}) async-start(bf16[4,64,1024]{2,1,0:T(8,128)(2,1)} %reshape.172), calls=%async_computation.6 | async-start | bytes 1048576 | tf_op jit(solution)/shard_map/all_to_all | solution.py:134
  132.7 1.8 copy-start.9
  134.5 1.7 copy-start.11
  134.5 1.7 copy-start.14
  162.4 30.1 %all-to-all-start.5 = ((bf16[4,64,1024]{2,1,0:T(8,128)(2,1)}), bf16[4,64,1024]{2,1,0:T(8,128)(2,1)}, u32[]{:S(2)}, u32[]{:S(2)}) async-start(bf16[4,64,1024]{2,1,0:T(8,128)(2,1)} %reshape.170), calls=%async_computation.5 | async-start | bytes 1048576 | tf_op jit(solution)/shard_map/all_to_all | solution.py:133
  184.1 3.8 %copy-start.5 = (bf16[256,8,128]{0,2,1:T(8,128)(2,1)S(1)}, bf16[256,8,128]{0,2,1:T(8,128)(2,1)}, u32[]{:S(2)}) copy-start(bf16[256,8,128]{0,2,1:T(8,128)(2,1)} %copy-done.4) | copy-start | bytes 1572868
  187.9 1.7 copy-start.7
  187.9 1.7 copy-start.15
  192.5 17.8 %all-to-all-start.3 = ((bf16[4,64,1024]{2,1,0:T(8,128)(2,1)}), bf16[4,64,1024]{2,1,0:T(8,128)(2,1)S(1)}, u32[]{:S(2)}, u32[]{:S(2)}) async-start(bf16[4,64,1024]{2,1,0:T(8,128)(2,1)} %reshape.166), calls=%async_computation.3 | async-start | bytes 1048576 | tf_op jit(solution)/shard_map/all_to_all | solution.py:132
Sparse Core Ops, SparseCore 0:
  54.9 61.5 all-gather.6
  118.1 65.9 all-gather.4
where the time goes:
time: 220 us; the launch traced here: 219 us
  waiting for transfers between devices  87.7 us (40%)
  blocking collectives  48.5 us (22%)
  local copies, waits for them, and re-layouts  21.6 us (10%)
  starting transfers between devices  19.6 us (9%)
  matrix products  14.6 us (7%)
  between operations  14.5 us (7%)
  other arithmetic  12.3 us (6%)
    all_to_all x1, blocking collectives, per_device(): lax.all_to_all(pack(keys), 'seq', split_axis=0, concat_axis=0, tiled=True)  27.9 us
    all_to_all x1, waiting for transfers between devices, per_device(): lax.all_to_all(pack(values), 'seq', split_axis=0, concat_axis=0, tiled=True)  25.5 us
    all_to_all x1, waiting for transfers between devices, per_device(): lax.all_to_all(to_slots(out_v), 'seq', split_axis=0, concat_axis=0, tiled...  21.8 us
    all_to_all x1, blocking collectives, per_device(): lax.all_to_all(pack(grad_output), 'seq', split_axis=0, concat_axis=0, til...  20.6 us
    all_gather x2, waiting for transfers between devices, entering(): pieces = lax.all_gather(value, axis)  17.4 us
    all_to_all x1, waiting for transfers between devices, per_device(): lax.all_to_all(pack(queries), 'seq', split_axis=0, concat_axis=0, tiled=T...  13.1 us
    all_to_all x1, waiting for transfers between devices, per_device(): lax.all_to_all(to_slots(out_q), 'seq', split_axis=0, concat_axis=0, tiled...  9.87 us
    select_n x6, other arithmetic, hop(): return jnp.where(position < mine, longer, total)  7.5 us
  transfers between devices with their start and end apart: 7, of which 5 were waited for; matrix products, arithmetic and copies ran while one was open for 16% of the time, Pallas kernels for 0%

commit v1 on v0

--- a/solution.py
+++ b/solution.py
@@ -6,6 +6,22 @@
 
 DH = 128
 highest = lax.Precision.HIGHEST
+
+
+def pairwise_exchange(array, axis, split, join):
+    ways, here = (lax.axis_size(axis), lax.axis_index(axis))
+    width = array.shape[split] // ways
+    dims = list(array.shape)
+    dims[split] = width
+    height = dims[join]
+    dims[join] = height * ways
+    full = jnp.zeros(dims, array.dtype)
+    for mask in range(ways):
+        part = lax.dynamic_slice_in_dim(array, (here ^ mask) * width, width, axis=split)
+        if mask:
+            part = lax.ppermute(part, axis, [(d, d ^ mask) for d in range(ways)])
+        full = lax.dynamic_update_slice_in_dim(full, part, (here ^ mask) * height, axis=join)
+    return full
 
 
 def entering(value, axis, join, neutral, backward):
@@ -57,7 +73,7 @@
     query_recv, key_recv, value_recv, grad_recv = (
         lax.all_to_all(pack(queries), "seq", split_axis=0, concat_axis=0, tiled=True),
         lax.all_to_all(pack(keys), "seq", split_axis=0, concat_axis=0, tiled=True),
-        lax.all_to_all(pack(values), "seq", split_axis=0, concat_axis=0, tiled=True),
+        pairwise_exchange(pack(values), "seq", 0, 0),
         lax.all_to_all(pack(grad_output), "seq", split_axis=0, concat_axis=0, tiled=True),
     )
     query_recv = split_heads(query_recv)

time: 220 us -> 221 us (level)
  blocking collectives: 48.5 us -> 20.6 us
  waiting for transfers between devices: 87.7 us -> 115 us
  starting transfers between devices: 19.6 us -> 23.4 us
    ppermute x0 -> x3, waiting for transfers between devices: none -> 35.6 us  [pairwise_exchange(): part = lax.ppermute(part, axis, [(d, d ^ mask) for d in range(ways)])]
    all_to_all x1 -> x0, blocking collectives: 27.9 us -> none  [per_device(): lax.all_to_all(pack(keys), 'seq', split_axis=0, concat_axis=0, tiled=True)]
    all_to_all x1, waiting for transfers between devices: 25.5 us -> 0.01 us  [per_device(): lax.all_to_all(pack(keys), 'seq', split_axis=0, concat_axis=0, tiled=True)]
    all_gather x2, waiting for transfers between devices: 17.4 us -> 34.5 us  [entering(): pieces = lax.all_gather(value, axis)]
    ppermute x0 -> x3, starting transfers between devices: none -> 4.45 us  [pairwise_exchange(): part = lax.ppermute(part, axis, [(d, d ^ mask) for d in range(ways)])]
  transfers between devices with their start and end apart: 7 -> 10, of which waited for: 5 -> 7; matrix products, arithmetic and copies ran while one was open for 16% -> 15% of each run, Pallas kernels for 0% -> 0%
where the time goes in v1:
time: 221 us; the launch traced here: 220 us
  waiting for transfers between devices  115 us (52%)
  starting transfers between devices  23.4 us (11%)
  local copies, waits for them, and re-layouts  21.5 us (10%)
  blocking collectives  20.6 us (9%)
  between operations  14.6 us (7%)
  matrix products  12.5 us (6%)
  other arithmetic  12.3 us (6%)
    ppermute x3, waiting for transfers between devices, pairwise_exchange(): part = lax.ppermute(part, axis, [(d, d ^ mask) for d in range(ways)])  35.6 us
    all_gather x2, waiting for transfers between devices, entering(): pieces = lax.all_gather(value, axis)  34.5 us
    all_to_all x1, waiting for transfers between devices, per_device(): lax.all_to_all(to_slots(out_v), 'seq', split_axis=0, concat_axis=0, tiled...  21.7 us
    all_to_all x1, blocking collectives, per_device(): lax.all_to_all(pack(grad_output), 'seq', split_axis=0, concat_axis=0, til...  20.6 us
    all_to_all x1, waiting for transfers between devices, per_device(): lax.all_to_all(pack(queries), 'seq', split_axis=0, concat_axis=0, tiled=T...  13.1 us
    all_to_all x1, waiting for transfers between devices, per_device(): lax.all_to_all(to_slots(out_q), 'seq', split_axis=0, concat_axis=0, tiled...  9.86 us
    select_n x6, other arithmetic, hop(): return jnp.where(position < mine, longer, total)  7.47 us
    gather x3, local copies, waits for them, and re-layouts, unpack(): jnp.take(returned.reshape(window_rows, width), source_index, axis=0)[None]  5.17 us
  transfers between devices with their start and end apart: 10, of which 7 were waited for; matrix products, arithmetic and copies ran while one was open for 15% of the time, Pallas kernels for 0%

profile of v1, /device:TPU:0, one launch (start us, length us, event | category | flops | bytes accessed | tf_op | source)
XLA Modules:
  0.0 219.7 jit_solution(9074986719932527272)
XLA Ops:
  7.2 0.8 iota_compare_fusion.3
  8.0 0.1 lt.103
  8.0 0.8 reduce-window.7
  8.9 0.7 bitcast_subtract_fusion
  9.5 0.1 iota_add_fusion
  9.6 0.1 add.133
  9.7 1.2 gather_fusion.4
  10.9 1.2 gather_fusion.1
  12.1 1.2 gather_fusion.2
  13.3 1.2 gather_fusion
  14.5 1.3 select_select_fusion
  15.8 20.6 %all_to_all.30 = bf16[4,64,1024]{2,1,0:T(8,128)(2,1)S(1)} all-to-all(bf16[4,64,1024]{2,1,0:T(8,128)(2,1)S(1)} %bitcast.71), channel_id=1, replica_groups=mesh['groups'=2,'seq'=4,'dp'=2,'mp'=2] {'seq'}, dimensions={0} | all-to-all | bytes 1048576 | tf_op jit(solution)/shard_map/all_to_all | solution.py:77
  36.4 3.5 %all-to-all-start.3 = ((bf16[4,64,1024]{2,1,0:T(8,128)(2,1)}), bf16[4,64,1024]{2,1,0:T(8,128)(2,1)S(1)}, u32[]{:S(2)}, u32[]{:S(2)}) async-start(bf16[4,64,1024]{2,1,0:T(8,128)(2,1)} %bitcast.14), calls=%async_computation.3 | async-start | bytes 1048576 | tf_op jit(solution)/shard_map/all_to_all | solution.py:74
  39.9 0.1 copy.71
  40.0 0.3 copy.66
  40.3 13.1 %all-to-all-done.3 = bf16[4,64,1024]{2,1,0:T(8,128)(2,1)S(1)} async-done(((bf16[4,64,1024]{2,1,0:T(8,128)(2,1)}), bf16[4,64,1024]{2,1,0:T(8,128)(2,1)S(1)}, u32[]{:S(2)}, u32[]{:S(2)}) %all-to-all-start.3) | async-done | bytes 524320 | tf_op jit(solution)/shard_map/all_to_all | solution.py:74
  53.5 0.1 copy.72
  53.6 1.2 fusion.47
  54.7 3.5 %all-to-all-start = ((bf16[4,64,1024]{2,1,0:T(8,128)(2,1)}), bf16[4,64,1024]{2,1,0:T(8,128)(2,1)S(1)}, u32[]{:S(2)}, u32[]{:S(2)}) async-start(bf16[4,64,1024]{2,1,0:T(8,128)(2,1)} %bitcast.4), calls=%async_computation | async-start | bytes 1048576 | tf_op jit(solution)/shard_map/all_to_all | solution.py:75
  58.4 2.0 collective-permute-start
  60.4 2.4 %collective-permute-start.1 = (bf16[1,64,1024]{2,1,0:T(8,128)(2,1)S(1)}, bf16[1,64,1024]{2,1,0:T(8,128)(2,1)S(1)}, u32[]{:S(2)}, u32[]{:S(2)}) collective-permute-start(bf16[1,64,1024]{2,1,0:T(8,128)(2,1)S(1)} %get-tuple-element.251), channel_id=1, source_target_pairs={{0,8},{4,12},{8,0},{12,4},{1,9},{5,13},{9,1},{13,5},{2,10},{6,14},... | collective-permute-start | bytes 393224 | tf_op jit(solution)/shard_map/ppermute | solution.py:22
  62.8 0.1 collective-permute-start.2
  62.9 16.4 %collective-permute-done = bf16[1,64,1024]{2,1,0:T(8,128)(2,1)S(1)} collective-permute-done((bf16[1,64,1024]{2,1,0:T(8,128)(2,1)S(1)}, bf16[1,64,1024]{2,1,0:T(8,128)(2,1)S(1)}, u32[]{:S(2)}, u32[]{:S(2)}) %collective-permute-start) | collective-permute-done | bytes 131104 | tf_op jit(solution)/shard_map/ppermute | solution.py:22
  79.3 19.2 %collective-permute-done.1 = bf16[1,64,1024]{2,1,0:T(8,128)(2,1)S(1)} collective-permute-done((bf16[1,64,1024]{2,1,0:T(8,128)(2,1)S(1)}, bf16[1,64,1024]{2,1,0:T(8,128)(2,1)S(1)}, u32[]{:S(2)}, u32[]{:S(2)}) %collective-permute-start.1) | collective-permute-done | bytes 131104 | tf_op jit(solution)/shard_map/ppermute | solution.py:22
  98.5 0.1 copy.70
  98.6 0.1 copy.69
  98.7 1.1 fusion.55
  100.0 1.8 fusion.49
  101.8 15.7 %all-gather.7.cloned.1.call-done = f32[32,128,128]{2,1,0:T(8,128)} async-done(((f32[8,128,128]{2,1,0:T(8,128)}), f32[32,128,128]{2,1,0:T(8,128)}) %all-gather.7.cloned.1.call-update) | async-done | bytes 2097168 | tf_op jit(solution)/shard_map/all_gather | solution.py:29
  117.5 3.2 %rev.3 = f32[4,8,128,128]{3,2,1,0:T(8,128)} reverse(f32[4,8,128,128]{3,2,1,0:T(8,128)} %bitcast.72), dimensions={0} | reverse | bytes 4194304 | tf_op jit(solution)/shard_map/rev | solution.py:31
  120.7 3.8 %while.35 = (s32[]{:T(128)}, f32[8,128,128]{2,1,0:T(8,128)S(1)}, s32[]{:T(128)}, f32[4,8,128,128]{3,2,1,0:T(8,128)}, s32[]{:T(128)}, /*index=5*/s32[]{:T(128)}) while((s32[]{:T(128)}, f32[8,128,128]{2,1,0:T(8,128)S(1)}, s32[]{:T(128)}, f32[4,8,128,128]{3,2,1,0:T(8,128)}, s32[]{:T(128)}, /*index=5*/s32[]{:T(128)}) %tuple.78), condition=%wide.region_6.9_spmd.clone, body=%wide.region_5.8_spmd.clone.sunk | while | flops 393220 | bytes 1572965 | solution.py:39
  120.7 1.3 add_select_fusion.5
  122.0 1.2 add_select_fusion.5
  123.3 1.2 add_select_fusion.5
  124.5 0.6 fusion.60
  125.2 1.1 copy-done.14
  126.3 1.1 fusion.39
  127.3 0.3 copy.67
  127.6 1.0 reshape.172
  128.7 4.1 %all-to-all-start.5 = ((bf16[4,64,1024]{2,1,0:T(8,128)(2,1)}), bf16[4,64,1024]{2,1,0:T(8,128)(2,1)}, u32[]{:S(2)}, u32[]{:S(2)}) async-start(bf16[4,64,1024]{2,1,0:T(8,128)(2,1)} %reshape.172), calls=%async_computation.5 | async-start | bytes 1048576 | tf_op jit(solution)/shard_map/all_to_all | solution.py:150
  132.8 1.8 fusion.53
  134.7 0.6 fusion.51
  135.3 0.4 copy-done.11
  135.7 1.2 fusion.36
  136.9 1.1 copy.61
  138.0 2.0 reshape.170
  140.1 21.7 %all-to-all-done.5 = bf16[4,64,1024]{2,1,0:T(8,128)(2,1)} async-done(((bf16[4,64,1024]{2,1,0:T(8,128)(2,1)}), bf16[4,64,1024]{2,1,0:T(8,128)(2,1)}, u32[]{:S(2)}, u32[]{:S(2)}) %all-to-all-start.5) | async-done | bytes 524320 | tf_op jit(solution)/shard_map/all_to_all | solution.py:150
  161.8 4.3 %all-to-all-start.4 = ((bf16[4,64,1024]{2,1,0:T(8,128)(2,1)}), bf16[4,64,1024]{2,1,0:T(8,128)(2,1)}, u32[]{:S(2)}, u32[]{:S(2)}) async-start(bf16[4,64,1024]{2,1,0:T(8,128)(2,1)} %reshape.170), calls=%async_computation.4 | async-start | bytes 1048576 | tf_op jit(solution)/shard_map/all_to_all | solution.py:149
  166.1 18.8 %all-gather.5.cloned.1.call-done = f32[32,128,128]{2,1,0:T(8,128)} async-done(((f32[8,128,128]{2,1,0:T(8,128)}), f32[32,128,128]{2,1,0:T(8,128)}) %all-gather.5.cloned.1.call-update) | async-done | bytes 2097168 | tf_op jit(solution)/shard_map/all_gather | solution.py:29
  184.9 3.8 %while.34 = (s32[]{:T(128)}, f32[8,128,128]{2,1,0:T(8,128)S(1)}, s32[]{:T(128)}, f32[4,8,128,128]{3,2,1,0:T(8,128)}, s32[]{:T(128)}, /*index=5*/s32[]{:T(128)}) while((s32[]{:T(128)}, f32[8,128,128]{2,1,0:T(8,128)S(1)}, s32[]{:T(128)}, f32[4,8,128,128]{3,2,1,0:T(8,128)}, s32[]{:T(128)}, /*index=5*/s32[]{:T(128)}) %tuple.88), condition=%wide.region_2.4_spmd.clone, body=%wide.region_1.3_spmd.clone.sunk | while | flops 393220 | bytes 1572965 | solution.py:39
  184.9 1.3 add_select_fusion.4
  186.2 1.2 add_select_fusion.4
  187.4 1.2 add_select_fusion.4
  188.7 1.7 fusion.45
  190.4 1.4 fusion.33
  191.9 0.3 copy.56
  192.2 1.0 reshape.166
  193.2 3.5 %all-to-all-start.2 = ((bf16[4,64,1024]{2,1,0:T(8,128)(2,1)}), bf16[4,64,1024]{2,1,0:T(8,128)(2,1)S(1)}, u32[]{:S(2)}, u32[]{:S(2)}) async-start(bf16[4,64,1024]{2,1,0:T(8,128)(2,1)} %reshape.166), calls=%async_computation.2 | async-start | bytes 1048576 | tf_op jit(solution)/shard_map/all_to_all | solution.py:148
  196.7 0.1 select_reduce_fusion.1
  196.8 2.2 gather_fusion.6
  199.0 2.2 gather_fusion.5
  201.1 9.9 %all-to-all-done.2 = bf16[4,64,1024]{2,1,0:T(8,128)(2,1)S(1)} async-done(((bf16[4,64,1024]{2,1,0:T(8,128)(2,1)}), bf16[4,64,1024]{2,1,0:T(8,128)(2,1)S(1)}, u32[]{:S(2)}, u32[]{:S(2)}) %all-to-all-start.2) | async-done | bytes 524320 | tf_op jit(solution)/shard_map/all_to_all | solution.py:148
  211.0 0.9 gather_fusion.3
  211.8 1.0 select_bitcast_fusion
  (53 shorter events, 0.5 us)
Async XLA Ops:
  7.2 2.5 %copy-start = (bf16[1,128,1024]{2,1,0:T(8,128)(2,1)S(1)}, bf16[1,128,1024]{2,1,0:T(8,128)(2,1)}, u32[]{:S(2)}) copy-start(bf16[1,128,1024]{2,1,0:T(8,128)(2,1)} %param.13) | copy-start | bytes 786436
  9.7 1.2 copy-start.1
  10.9 1.2 copy-start.2
  12.1 1.2 copy-start.3
  36.4 17.1 %all-to-all-start.3 = ((bf16[4,64,1024]{2,1,0:T(8,128)(2,1)}), bf16[4,64,1024]{2,1,0:T(8,128)(2,1)S(1)}, u32[]{:S(2)}, u32[]{:S(2)}) async-start(bf16[4,64,1024]{2,1,0:T(8,128)(2,1)} %bitcast.14), calls=%async_computation.3 | async-start | bytes 1048576 | tf_op jit(solution)/shard_map/all_to_all | solution.py:74
  39.9 77.6 %all-gather.7.cloned.1.call-start = ((), (), s32[]{:S(2)}) async-start(), calls=%async_computation.7 | async-start | bytes 2621440 | tf_op jit(solution)/shard_map/all_gather | solution.py:29
  40.3 84.8 %copy-start.4 = (bf16[256,8,128]{0,2,1:T(8,128)(2,1)}, bf16[256,8,128]{0,2,1:T(8,128)(2,1)S(1)}, u32[]{:S(2)}) copy-start(bf16[256,8,128]{0,2,1:T(8,128)(2,1)S(1)} %copy.66) | copy-start | bytes 1572868
  53.6 46.4 %copy-start.10 = (bf16[32,8,8,128]{3,2,1,0:T(8,128)(2,1)}, bf16[32,8,8,128]{3,2,1,0:T(8,128)(2,1)S(1)}, u32[]{:S(2)}) copy-start(bf16[32,8,8,128]{3,2,1,0:T(8,128)(2,1)S(1)} %copy.72) | copy-start | bytes 1572868
  54.7 43.9 %all-to-all-start = ((bf16[4,64,1024]{2,1,0:T(8,128)(2,1)}), bf16[4,64,1024]{2,1,0:T(8,128)(2,1)S(1)}, u32[]{:S(2)}, u32[]{:S(2)}) async-start(bf16[4,64,1024]{2,1,0:T(8,128)(2,1)} %bitcast.4), calls=%async_computation | async-start | bytes 1048576 | tf_op jit(solution)/shard_map/all_to_all | solution.py:75
  58.2 126.6 %all-gather.5.cloned.1.call-start = ((), (), s32[]{:S(2)}) async-start(), calls=%async_computation.6 | async-start | bytes 2621440 | tf_op jit(solution)/shard_map/all_gather | solution.py:29
  58.4 20.8 %collective-permute-start = (bf16[1,64,1024]{2,1,0:T(8,128)(2,1)S(1)}, bf16[1,64,1024]{2,1,0:T(8,128)(2,1)S(1)}, u32[]{:S(2)}, u32[]{:S(2)}) collective-permute-start(bf16[1,64,1024]{2,1,0:T(8,128)(2,1)S(1)} %get-tuple-element.252), channel_id=1, source_target_pairs={{0,4},{4,0},{8,12},{12,8},{1,5},{5,1},{9,13},{13,9},{2,6},{6,2},{1... | collective-permute-start | bytes 393224 | tf_op jit(solution)/shard_map/ppermute | solution.py:22
  60.4 38.0 %collective-permute-start.1 = (bf16[1,64,1024]{2,1,0:T(8,128)(2,1)S(1)}, bf16[1,64,1024]{2,1,0:T(8,128)(2,1)S(1)}, u32[]{:S(2)}, u32[]{:S(2)}) collective-permute-start(bf16[1,64,1024]{2,1,0:T(8,128)(2,1)S(1)} %get-tuple-element.251), channel_id=1, source_target_pairs={{0,8},{4,12},{8,0},{12,4},{1,9},{5,13},{9,1},{13,5},{2,10},{6,14},... | collective-permute-start | bytes 393224 | tf_op jit(solution)/shard_map/ppermute | solution.py:22
  62.8 35.7 %collective-permute-start.2 = (bf16[1,64,1024]{2,1,0:T(8,128)(2,1)S(1)}, bf16[1,64,1024]{2,1,0:T(8,128)(2,1)S(1)}, u32[]{:S(2)}, u32[]{:S(2)}) collective-permute-start(bf16[1,64,1024]{2,1,0:T(8,128)(2,1)S(1)} %get-tuple-element.250), channel_id=1, source_target_pairs={{0,12},{4,8},{8,4},{12,0},{1,13},{5,9},{9,5},{13,1},{2,14},{6,10},... | collective-permute-start | bytes 393224 | tf_op jit(solution)/shard_map/ppermute | solution.py:22
  98.6 1.3 copy-start.12
  98.7 25.8 %copy-start.6 = (bf16[32,8,8,128]{3,2,1,0:T(8,128)(2,1)}, bf16[32,8,8,128]{3,2,1,0:T(8,128)(2,1)S(1)}, u32[]{:S(2)}) copy-start(bf16[32,8,8,128]{3,2,1,0:T(8,128)(2,1)S(1)} %copy.69) | copy-start | bytes 1572868
  100.0 25.2 %copy-start.15 = (f32[256,256]{1,0:T(8,128)}, f32[256,256]{1,0:T(8,128)S(1)}, u32[]{:S(2)}) copy-start(f32[256,256]{1,0:T(8,128)S(1)} %fusion.62) | copy-start | bytes 786436
  120.7 3.8 %copy-start.8 = (f32[8,128,128]{2,1,0:T(8,128)S(1)}, f32[8,128,128]{2,1,0:T(8,128)}, u32[]{:S(2)}) copy-start(f32[8,128,128]{2,1,0:T(8,128)} %fusion.47) | copy-start | bytes 1572868
  124.5 1.7 copy-start.14
  128.7 33.1 %all-to-all-start.5 = ((bf16[4,64,1024]{2,1,0:T(8,128)(2,1)}), bf16[4,64,1024]{2,1,0:T(8,128)(2,1)}, u32[]{:S(2)}, u32[]{:S(2)}) async-start(bf16[4,64,1024]{2,1,0:T(8,128)(2,1)} %reshape.172), calls=%async_computation.5 | async-start | bytes 1048576 | tf_op jit(solution)/shard_map/all_to_all | solution.py:150
  132.8 1.8 copy-start.9
  132.8 1.8 copy-start.13
  134.6 1.0 copy-start.11
  134.6 1.1 copy-start.16
  161.8 31.4 %all-to-all-start.4 = ((bf16[4,64,1024]{2,1,0:T(8,128)(2,1)}), bf16[4,64,1024]{2,1,0:T(8,128)(2,1)}, u32[]{:S(2)}, u32[]{:S(2)}) async-start(bf16[4,64,1024]{2,1,0:T(8,128)(2,1)} %reshape.170), calls=%async_computation.4 | async-start | bytes 1048576 | tf_op jit(solution)/shard_map/all_to_all | solution.py:149
  184.9 3.8 %copy-start.5 = (bf16[256,8,128]{0,2,1:T(8,128)(2,1)S(1)}, bf16[256,8,128]{0,2,1:T(8,128)(2,1)}, u32[]{:S(2)}) copy-start(bf16[256,8,128]{0,2,1:T(8,128)(2,1)} %copy-done.4) | copy-start | bytes 1572868
  188.7 1.7 copy-start.7
  188.7 1.7 copy-start.17
  193.2 17.8 %all-to-all-start.2 = ((bf16[4,64,1024]{2,1,0:T(8,128)(2,1)}), bf16[4,64,1024]{2,1,0:T(8,128)(2,1)S(1)}, u32[]{:S(2)}, u32[]{:S(2)}) async-start(bf16[4,64,1024]{2,1,0:T(8,128)(2,1)} %reshape.166), calls=%async_computation.2 | async-start | bytes 1048576 | tf_op jit(solution)/shard_map/all_to_all | solution.py:148
Sparse Core Ops, SparseCore 0:
  54.9 62.5 all-gather.6
  119.1 65.7 all-gather.4
